TPU v7x, 32 devices: a whole 2x2x4 slice. The times are simulated.
32 devices in a mesh: groups: 2 (over x), dev: 16 (over z, y, core).
Axes of the slice: x: 2, y: 2, z: 4, core: 2. Of those that a mesh axis runs over, the one named last changes fastest.
Arguments:
- queries: bfloat16 [2, 32, 128, 1024], P(None, ('groups', 'dev')), parts along dimension 1, may hold values from -180 to 180
- keys_values: bfloat16 [2, 32, 2, 1664, 128], P(None, ('groups', 'dev')), parts along dimension 1, may hold values from -6 to 6
- residual: bfloat16 [2, 2048, 2048], P(None, ('groups', 'dev')), parts along dimension 1, may hold values from -6 to 6
- norm_gain: float32 [2048], replicated, may hold values from 0.1 to 1.9
- gate_up: bfloat16 [16, 2048, 1536], P('dev'), may hold values from -0.125 to 0.125
- down_proj: bfloat16 [16, 768, 2048], P('dev'), may hold values from -0.21875 to 0.21875
- expert_ids: int32 [2, 2048, 8], P(None, ('groups', 'dev')), parts along dimension 1, may hold values from 0 to 15, all different within a row; in each aligned block of 64 rows (0 to 63, 64 to 127, ..., all dimensions but the last counted through in order) at most 40 rows name the same one
- expert_gates: int32 [2, 2048, 8], P(None, ('groups', 'dev')), parts along dimension 1, may hold values from 1 to 1023
Outputs:
- layer_out: bfloat16 [2, 2048, 2048], P(None, ('groups', 'dev')), parts along dimension 1
There are 2 independent parts, one for each index of `groups`. A program takes and returns all parts, laid end to end along the dimension named above; an argument that names none is the same for every part. Nothing has to cross between parts.
Inputs may be any that keep to these rules, and one draw needn't show every extreme that they name: `expert_ids`: in each micro-batch and each aligned block of 64 rows (the tokens of one device), no expert is named by more than 40 rows, a bound that some block reaches; the 8 experts of a row differ.
All inputs are finite; a program needn't handle non-finite values.
Results may differ from a plain program's by a relative error of at most 0.0039.
Values may be sent and summed in bfloat16 or wider, within the bound.
A program may use at most 128 MiB of HBM per device.

v0:
```python
import math
import jax
import jax.numpy as jnp
from jax import lax
from jax.sharding import PartitionSpec as P


def attend(query_rows, cached_pairs):
    batches, length, feat_width = query_rows.shape
    context = cached_pairs.shape[2]
    head_size = cached_pairs.shape[3]
    groups = feat_width // head_size
    head_rows = query_rows.reshape(batches, length, groups, head_size)
    scores = jnp.einsum(
        "mqgd,mkd->mgqk", head_rows, cached_pairs[:, 0], preferred_element_type=jnp.float32
    ) / math.sqrt(head_size)
    query_pos = context - length + lax.broadcasted_iota(jnp.int32, (length, context), 0)
    key_pos = lax.broadcasted_iota(jnp.int32, (length, context), 1)
    allowed = key_pos <= query_pos
    scores = jnp.where(allowed, scores, -1e30)
    highest = jnp.max(scores, axis=-1, keepdims=True)
    scaled_exp = jnp.where(allowed, jnp.exp(scores - highest), 0.0)
    totals = jnp.sum(scaled_exp, axis=-1, keepdims=True)
    weights = (scaled_exp / totals).astype(jnp.bfloat16)
    blended = jnp.einsum(
        "mgqk,mkd->mqgd", weights, cached_pairs[:, 1], preferred_element_type=jnp.float32
    )
    return blended.astype(jnp.bfloat16).reshape(batches, length, feat_width)


def to_owners(exchanged, kv_heads):
    batches, sources, positions, feat_width = exchanged.shape
    grouped = exchanged.reshape(batches, sources // kv_heads, kv_heads, positions, feat_width)
    grouped = jnp.transpose(grouped, (0, 1, 3, 2, 4))
    return grouped.reshape(batches, sources // kv_heads * positions, kv_heads * feat_width)


def prepare(attn_rows, residual, norm_gain):
    stream = residual.astype(jnp.float32) + attn_rows.astype(jnp.float32)
    meansq = jnp.mean(stream * stream, axis=-1, keepdims=True)
    normed = (stream * lax.rsqrt(meansq + 1e-06) * norm_gain).astype(jnp.bfloat16)
    return (stream, normed)


def dense_shares(expert_ids, expert_gates, experts):
    shares = expert_gates.astype(jnp.float32)
    shares = shares / jnp.sum(shares, axis=-1, keepdims=True)
    named = expert_ids[..., None] == jnp.arange(experts, dtype=jnp.int32)
    return jnp.sum(jnp.where(named, shares[..., None], 0.0), axis=-2)


def run_expert(rows_in, gate_up, down_proj, weight):
    hidden_width = down_proj.shape[1]
    projected = jnp.dot(rows_in, gate_up[0], preferred_element_type=jnp.float32)
    hidden = (jax.nn.silu(projected[:, :hidden_width]) * projected[:, hidden_width:]).astype(
        jnp.bfloat16
    )
    output = jnp.dot(hidden, down_proj[0], preferred_element_type=jnp.float32)
    return (output * weight).astype(jnp.bfloat16)


def body(queries, keys_values, residual, norm_gain, gate_up, down_proj, expert_ids, expert_gates):
    devices = lax.axis_size("dev")
    me = lax.axis_index("dev")
    model_width = residual.shape[2]
    kv_heads = model_width // queries.shape[3]
    experts = devices * gate_up.shape[0]
    own_query = queries[:, 0]
    own_pairs = keys_values[:, 0]
    batches, length, feat_width = own_query.shape
    positions = length // devices
    weights = dense_shares(expert_ids, expert_gates, experts)
    weights = lax.all_gather(weights, "dev", axis=1, tiled=True)
    mine = jnp.sum(
        jnp.where(jnp.arange(experts, dtype=jnp.int32) == me, weights, 0.0), axis=-1, keepdims=True
    )
    pieces = []
    for batch_index in range(batches):
        window = slice(batch_index, batch_index + 1)
        blended_heads = attend(own_query[window], own_pairs[window])
        outgoing_rows = blended_heads.reshape(1, devices, positions, feat_width)
        arrived_rows = lax.all_to_all(outgoing_rows, "dev", split_axis=1, concat_axis=1, tiled=True)
        attn_rows = to_owners(arrived_rows, kv_heads)
        stream, normed = prepare(attn_rows[0], residual[batch_index], norm_gain)
        rows_in = lax.all_gather(normed, "dev", axis=0, tiled=True)
        partial = run_expert(rows_in, gate_up, down_proj, mine[batch_index])
        summed = lax.psum_scatter(partial, "dev", scatter_dimension=0, tiled=True)
        pieces.append((stream + summed.astype(jnp.float32)).astype(jnp.bfloat16))
    return jnp.stack(pieces, axis=0)


def solution(mesh):
    in_specs = (
        P(None, ("groups", "dev"), None, None),
        P(None, ("groups", "dev"), None, None, None),
        P(None, ("groups", "dev"), None),
        P(),
        P("dev", None, None),
        P("dev", None, None),
        P(None, ("groups", "dev"), None),
        P(None, ("groups", "dev"), None),
    )
    out_specs = P(None, ("groups", "dev"), None)
    return jax.shard_map(body, mesh=mesh, in_specs=in_specs, out_specs=out_specs, check_vma=False)
```

profile of v0, /device:TPU:0, one launch (start us, length us, event | category | flops | bytes accessed | tf_op | source)
XLA Modules:
  0.0 324.2 jit_solution(8820558559050557088)
XLA Ops:
  6.7 2.9 slice_bitcast_fusion
  9.6 1.8 fusion.50
  11.4 1.8 copy.62
  13.2 1.8 copy.64
  15.0 2.3 fusion.4
  17.3 2.8 fusion.6
  20.1 1.6 fusion.7
  21.7 2.6 fusion.26
  24.3 0.9 copy.55
  25.2 1.8 reshape_reshape.7
  26.9 7.5 %all-to-all-start.1 = ((bf16[1,16,8,1024]{3,2,0,1:T(8,128)(2,1)}), bf16[1,16,8,1024]{3,2,0,1:T(8,128)(2,1)}, u32[]{:S(2)}, u32[]{:S(2)}) async-start(bf16[1,16,8,1024]{3,2,0,1:T(8,128)(2,1)} %bitcast.156), calls=%async_computation.2 | async-start | bytes 524288 | tf_op jit(solution)/shard_map/all_to_all | solution.py:82
  34.4 5.5 %fusion.29 = bf16[1,128,8,128]{3,1,2,0:T(8,128)(2,1)S(1)} fusion(f32[8,128]{1,0:T(8,128)S(1)} %get-tuple-element.7, f32[8,128]{1,0:T(8,128)S(1)} %get-tuple-element.19, f32[1664,128,8]{1,0,2:T(8,128)} %copy-done.1, pred[128,1664]{0,1:T(8,128)(4,1)S(1)} %iota_compare_fusion, bf16[1,2,1664,128]{3,2,1,0:T(8,128)(2,1)} %get-tuple-element.10), kind=kOutput, calls=%fused_computation.31 | convolution fusion | flops 446562304 | bytes 7725056 | tf_op jit(solution)/shard_map/mgqk,mkd->mqgd/dot_general | solution.py:25
  41.0 3.5 %all-to-all-done.1 = bf16[1,16,8,1024]{3,2,0,1:T(8,128)(2,1)} async-done(((bf16[1,16,8,1024]{3,2,0,1:T(8,128)(2,1)}), bf16[1,16,8,1024]{3,2,0,1:T(8,128)(2,1)}, u32[]{:S(2)}, u32[]{:S(2)}) %all-to-all-start.1) | async-done | bytes 262176 | tf_op jit(solution)/shard_map/all_to_all | solution.py:82
  44.5 3.5 %all-to-all-start = ((bf16[1,16,8,1024]{3,2,0,1:T(8,128)(2,1)}), bf16[1,16,8,1024]{3,2,0,1:T(8,128)(2,1)S(1)}, u32[]{:S(2)}, u32[]{:S(2)}) async-start(bf16[1,16,8,1024]{3,2,0,1:T(8,128)(2,1)} %bitcast.157), calls=%async_computation | async-start | bytes 524288 | tf_op jit(solution)/shard_map/all_to_all | solution.py:82
  48.3 1.8 convert.11
  50.1 7.9 %all-to-all-done = bf16[1,16,8,1024]{3,2,0,1:T(8,128)(2,1)S(1)} async-done(((bf16[1,16,8,1024]{3,2,0,1:T(8,128)(2,1)}), bf16[1,16,8,1024]{3,2,0,1:T(8,128)(2,1)S(1)}, u32[]{:S(2)}, u32[]{:S(2)}) %all-to-all-start) | async-done | bytes 262176 | tf_op jit(solution)/shard_map/all_to_all | solution.py:82
  58.1 1.6 multiply_reduce_fusion.1
  59.7 2.2 multiply_convert_fusion.3
  62.9 24.2 %all_gather.10 = f32[2,1024,16]{2,0,1:T(2,128)S(1)} all-gather(f32[2,64,16]{2,0,1:T(2,128)S(1)} %copy.50), channel_id=1, replica_groups=mesh['groups'=2,'dev'=16] {'dev'}, dimensions={1}, use_global_device_ids=true | all-gather | bytes 139264 | tf_op jit(solution)/shard_map/all_gather | solution.py:73
  87.1 1.2 select_reduce_fusion
  88.3 1.1 fusion.49
  89.4 1.3 copy.65
  90.7 22.6 %all-gather.5.cloned.1.call-done = bf16[1024,2048]{1,0:T(8,128)(2,1)} async-done(((bf16[64,2048]{1,0:T(8,128)(2,1)}), bf16[1024,2048]{1,0:T(8,128)(2,1)}) %all-gather.5.cloned.1.call-update) | async-done | bytes 4194320 | tf_op jit(solution)/shard_map/all_gather | solution.py:85
  113.3 10.0 %fusion = f32[1024,1536]{1,0:T(8,128)S(1)} fusion(bf16[1024,2048]{1,0:T(8,128)(2,1)} %all-gather.5.cloned.1.call-done, bf16[1,2048,1536]{2,1,0:T(8,128)(2,1)} %param.12), kind=kOutput, calls=%fused_computation.8 | convolution fusion | flops 6442450944 | bytes 16777216 | tf_op jit(solution)/shard_map/dot_general | solution.py:54
  123.4 5.1 %multiply_convert_fusion = bf16[1024,2048]{1,0:T(8,128)(2,1)} fusion(f32[1024]{0:T(1024)S(1)} %bitcast.159, bf16[1,768,2048]{2,1,0:T(8,128)(2,1)S(1)} %copy-done, f32[1024,1536]{1,0:T(8,128)S(1)} %fusion), kind=kOutput, calls=%fused_computation | convolution fusion | flops 3230138368 | bytes 13635584 | tf_op jit(solution)/shard_map/dot_general | solution.py:58
  128.5 1.2 copy.63
  129.7 34.7 %all-gather.3.cloned.1.call-done = bf16[1024,2048]{1,0:T(8,128)(2,1)} async-done(((bf16[64,2048]{1,0:T(8,128)(2,1)}), bf16[1024,2048]{1,0:T(8,128)(2,1)}) %all-gather.3.cloned.1.call-update) | async-done | bytes 4194320 | tf_op jit(solution)/shard_map/all_gather | solution.py:85
  164.4 10.0 %fusion.2 = f32[1024,1536]{1,0:T(8,128)S(1)} fusion(bf16[1024,2048]{1,0:T(8,128)(2,1)} %all-gather.3.cloned.1.call-done, bf16[1,2048,1536]{2,1,0:T(8,128)(2,1)} %param.12), kind=kOutput, calls=%fused_computation.10 | convolution fusion | flops 6442450944 | bytes 16777216 | tf_op jit(solution)/shard_map/dot_general | solution.py:54
  174.4 5.1 %multiply_convert_fusion.1 = bf16[1024,2048]{1,0:T(8,128)(2,1)} fusion(f32[1024]{0:T(1024)S(1)} %bitcast.160, bf16[1,768,2048]{2,1,0:T(8,128)(2,1)S(1)} %copy-done, f32[1024,1536]{1,0:T(8,128)S(1)} %fusion.2), kind=kOutput, calls=%fused_computation.1 | convolution fusion | flops 3230138368 | bytes 13635584 | tf_op jit(solution)/shard_map/dot_general | solution.py:58
  179.5 60.1 %reduce-scatter.5.cloned.1.call-done = bf16[64,2048]{1,0:T(8,128)(2,1)} async-done(((bf16[1024,2048]{1,0:T(8,128)(2,1)}), bf16[64,2048]{1,0:T(8,128)(2,1)}) %reduce-scatter.5.cloned.1.call-update) | async-done | bytes 262160 | tf_op jit(solution)/shard_map/reduce_scatter | solution.py:87
  239.6 75.5 %reduce-scatter.3.cloned.1.call-done = bf16[64,2048]{1,0:T(8,128)(2,1)} async-done(((bf16[1024,2048]{1,0:T(8,128)(2,1)}), bf16[64,2048]{1,0:T(8,128)(2,1)}) %reduce-scatter.3.cloned.1.call-update) | async-done | bytes 262160 | tf_op jit(solution)/shard_map/reduce_scatter | solution.py:87
  315.2 2.5 fusion.34
  (35 shorter events, 2.5 us)
Async XLA Ops:
  6.5 116.8 %copy-start = (bf16[1,768,2048]{2,1,0:T(8,128)(2,1)S(1)}, bf16[1,768,2048]{2,1,0:T(8,128)(2,1)}, u32[]{:S(2)}) copy-start(bf16[1,768,2048]{2,1,0:T(8,128)(2,1)} %param.13) | copy-start | bytes 9437188
  15.0 2.3 copy-start.3
  15.0 2.3 copy-start.4
  17.3 2.8 copy-start.1
  26.9 17.5 %all-to-all-start.1 = ((bf16[1,16,8,1024]{3,2,0,1:T(8,128)(2,1)}), bf16[1,16,8,1024]{3,2,0,1:T(8,128)(2,1)}, u32[]{:S(2)}, u32[]{:S(2)}) async-start(bf16[1,16,8,1024]{3,2,0,1:T(8,128)(2,1)} %bitcast.156), calls=%async_computation.2 | async-start | bytes 524288 | tf_op jit(solution)/shard_map/all_to_all | solution.py:82
  34.4 25.3 %copy-start.5 = (f32[2048]{0:T(1024)S(1)}, f32[2048]{0:T(1024)}, u32[]{:S(2)}) copy-start(f32[2048]{0:T(1024)} %param.11) | copy-start | bytes 24580
  39.9 22.8 %copy-start.7 = (s32[2,64,8]{1,2,0:T(8,128)S(1)}, s32[2,64,8]{1,2,0:T(8,128)}, u32[]{:S(2)}) copy-start(s32[2,64,8]{1,2,0:T(8,128)} %param.15) | copy-start | bytes 12292
  40.0 22.8 %copy-start.6 = (s32[2,64,8]{1,2,0:T(8,128)S(1)}, s32[2,64,8]{1,2,0:T(8,128)}, u32[]{:S(2)}) copy-start(s32[2,64,8]{1,2,0:T(8,128)} %param.14) | copy-start | bytes 12292
  44.5 13.5 %all-to-all-start = ((bf16[1,16,8,1024]{3,2,0,1:T(8,128)(2,1)}), bf16[1,16,8,1024]{3,2,0,1:T(8,128)(2,1)S(1)}, u32[]{:S(2)}, u32[]{:S(2)}) async-start(bf16[1,16,8,1024]{3,2,0,1:T(8,128)(2,1)} %bitcast.157), calls=%async_computation | async-start | bytes 524288 | tf_op jit(solution)/shard_map/all_to_all | solution.py:82
  48.0 65.3 %all-gather.5.cloned.1.call-start = ((), (), s32[]{:S(2)}) async-start(), calls=%async_computation.6 | async-start | bytes 4456448 | tf_op jit(solution)/shard_map/all_gather | solution.py:85
  58.1 1.7 copy-start.2
  61.9 102.5 %all-gather.3.cloned.1.call-start = ((), (), s32[]{:S(2)}) async-start(), calls=%async_computation.4 | async-start | bytes 4456448 | tf_op jit(solution)/shard_map/all_gather | solution.py:85
  62.7 177.0 %reduce-scatter.5.cloned.1.call-start = ((), (), s32[]{:S(2)}) async-start(), calls=%async_computation.7 | async-start | bytes 4456448 | tf_op jit(solution)/shard_map/reduce_scatter | solution.py:87
  128.5 186.7 %reduce-scatter.3.cloned.1.call-start = ((), (), s32[]{:S(2)}) async-start(), calls=%async_computation.5 | async-start | bytes 4456448 | tf_op jit(solution)/shard_map/reduce_scatter | solution.py:87
Sparse Core Ops, SparseCore 0:
  62.0 51.2 all-gather.4
  115.5 48.8 all-gather.2
  168.3 71.2 reduce-scatter.4
  243.3 71.7 reduce-scatter.2
where the time goes:
time: 325 us; the launch traced here: 324 us
  waiting for transfers between devices  205 us (63%)
  matrix products  43.3 us (13%)
  blocking collectives  24.2 us (7%)
  local copies, waits for them, and re-layouts  15.7 us (5%)
  between operations  13.4 us (4%)
  starting transfers between devices  11.3 us (3%)
  other arithmetic  11.2 us (3%)
    reduce_scatter x2, waiting for transfers between devices, body(): summed = lax.psum_scatter(partial, 'dev', scatter_dimension=0, tiled=True)  136 us
    all_gather x2, waiting for transfers between devices, body(): rows_in = lax.all_gather(normed, 'dev', axis=0, tiled=True)  57.3 us
    all_gather x1, blocking collectives, body(): weights = lax.all_gather(weights, 'dev', axis=1, tiled=True)  24.2 us
    dot_general x2, matrix products, run_expert(): projected = jnp.dot(rows_in, gate_up[0], preferred_element_type=jnp.float32)  20 us
    all_to_all x2, waiting for transfers between devices, body(): lax.all_to_all(outgoing_rows, 'dev', split_axis=1, concat_axis=1, tiled=T...  11.4 us
    all_to_all x2, starting transfers between devices, body(): lax.all_to_all(outgoing_rows, 'dev', split_axis=1, concat_axis=1, tiled=T...  11 us
    dot_general x2, matrix products, run_expert(): output = jnp.dot(hidden, down_proj[0], preferred_element_type=jnp.float32)  10.1 us
    dot_general x2, matrix products, attend(): jnp.einsum('mgqk,mkd->mqgd', weights, cached_pairs[:, 1], preferred_eleme...  8.07 us
  transfers between devices with their start and end apart: 6, of which 6 were waited for; matrix products, arithmetic and copies ran while one was open for 13% of the time, Pallas kernels for 0%

commit v1 on v0

--- a/solution.py
+++ b/solution.py
@@ -3,6 +3,22 @@
 import jax.numpy as jnp
 from jax import lax
 from jax.sharding import PartitionSpec as P
+
+
+def use_turns(my_data):
+    named_axis = "dev"
+    trail = [my_data]
+    n_blocks = lax.axis_size(named_axis)
+    to_i = 1
+    while to_i < n_blocks:
+        reached = lax.ppermute(
+            trail[to_i - 1], named_axis, [(w, (w - 1) % n_blocks) for w in range(n_blocks)]
+        )
+        trail.append(reached)
+        to_i += 1
+    y2 = jnp.concatenate(trail, axis=0)
+    f_now = lax.axis_index(named_axis)
+    return jnp.roll(y2, f_now * my_data.shape[0], axis=0)
 
 
 def attend(query_rows, cached_pairs):
@@ -82,7 +98,7 @@
         arrived_rows = lax.all_to_all(outgoing_rows, "dev", split_axis=1, concat_axis=1, tiled=True)
         attn_rows = to_owners(arrived_rows, kv_heads)
         stream, normed = prepare(attn_rows[0], residual[batch_index], norm_gain)
-        rows_in = lax.all_gather(normed, "dev", axis=0, tiled=True)
+        rows_in = use_turns(normed)
         partial = run_expert(rows_in, gate_up, down_proj, mine[batch_index])
         summed = lax.psum_scatter(partial, "dev", scatter_dimension=0, tiled=True)
         pieces.append((stream + summed.astype(jnp.float32)).astype(jnp.bfloat16))

time: 325 us -> 388 us (1.19)
  starting transfers between devices: 11.3 us -> 111 us
  waiting for transfers between devices: 205 us -> 126 us
  local copies, waits for them, and re-layouts: 15.7 us -> 53.3 us
    ppermute x0 -> x30, starting transfers between devices: none -> 97.9 us  [use_turns(): lax.ppermute(trail[to_i - 1], named_axis, [(w, (w - 1) % n_blocks) for w...]
    reduce_scatter x2, waiting for transfers between devices: 136 us -> 75.8 us  [body(): summed = lax.psum_scatter(partial, 'dev', scatter_dimension=0, tiled=True)]
    all_gather x2 -> x0, waiting for transfers between devices: 57.3 us -> none  [body(): rows_in = lax.all_gather(normed, 'dev', axis=0, tiled=True)]
    ppermute x0 -> x30, waiting for transfers between devices: none -> 41.9 us  [use_turns(): lax.ppermute(trail[to_i - 1], named_axis, [(w, (w - 1) % n_blocks) for w...]
    unnamed x20 -> x60, local copies, waits for them, and re-layouts: 6.13 us -> 43.4 us
  transfers between devices with their start and end apart: 6 -> 34, of which waited for: 6 -> 20; matrix products, arithmetic and copies ran while one was open for 13% -> 22% of each run, Pallas kernels for 0% -> 0%
where the time goes in v1:
time: 388 us; the launch traced here: 386 us
  waiting for transfers between devices  126 us (32%)
  starting transfers between devices  111 us (29%)
  local copies, waits for them, and re-layouts  53.3 us (14%)
  matrix products  44.2 us (11%)
  blocking collectives  23.8 us (6%)
  other arithmetic  14.3 us (4%)
  between operations  13.7 us (4%)
    ppermute x30, starting transfers between devices, use_turns(): lax.ppermute(trail[to_i - 1], named_axis, [(w, (w - 1) % n_blocks) for w...  97.9 us
    reduce_scatter x2, waiting for transfers between devices, body(): summed = lax.psum_scatter(partial, 'dev', scatter_dimension=0, tiled=True)  75.8 us
    unnamed x60, local copies, waits for them, and re-layouts  43.4 us
    ppermute x30, waiting for transfers between devices, use_turns(): lax.ppermute(trail[to_i - 1], named_axis, [(w, (w - 1) % n_blocks) for w...  41.9 us
    all_gather x1, blocking collectives, body(): weights = lax.all_gather(weights, 'dev', axis=1, tiled=True)  23.8 us
    dot_general x2, matrix products, run_expert(): projected = jnp.dot(rows_in, gate_up[0], preferred_element_type=jnp.float32)  20.8 us
    all_to_all x2, starting transfers between devices, body(): lax.all_to_all(outgoing_rows, 'dev', split_axis=1, concat_axis=1, tiled=T...  12.9 us
    dot_general x2, matrix products, run_expert(): output = jnp.dot(hidden, down_proj[0], preferred_element_type=jnp.float32)  10.3 us
  transfers between devices with their start and end apart: 34, of which 20 were waited for; matrix products, arithmetic and copies ran while one was open for 22% of the time, Pallas kernels for 0%

profile of v1, /device:TPU:0, one launch (start us, length us, event | category | flops | bytes accessed | tf_op | source)
XLA Modules:
  0.0 386.4 jit_solution(1999528252751871929)
XLA Ops:
  16.2 4.6 %fusion.6 = (f32[8,128]{1,0:T(8,128)S(1)}, f32[8,128]{1,0:T(8,128)S(1)}, f32[1664,128,8]{1,0,2:T(8,128)}) fusion(f32[1664,128,8]{1,0,2:T(8,128)S(1)} %get-tuple-element.25, f32[8,128]{1,0:T(8,128)S(1)} %get-tuple-element.24, pred[128,1664]{0,1:T(8,128)(4,1)S(1)} %iota_compare_fusion, bf16[128,8,128]{0,2,1:T(8,128)(2,1)S(1)} %bitcast.158, ...), kind=kOutput, calls=%fused_computation.18 | convolution fusion | flops 449837056 | bytes 14544896 | tf_op jit(solution)/shard_map/mqgd,mkd->mgqk/dot_general | solution.py:30
  26.0 7.5 %all-to-all-start = ((bf16[1,16,8,1024]{3,2,0,1:T(8,128)(2,1)}), bf16[1,16,8,1024]{3,2,0,1:T(8,128)(2,1)}, u32[]{:S(2)}, u32[]{:S(2)}) async-start(bf16[1,16,8,1024]{3,2,0,1:T(8,128)(2,1)} %bitcast.156), calls=%async_computation | async-start | bytes 524288 | tf_op jit(solution)/shard_map/all_to_all | solution.py:98
  33.5 4.7 %fusion.7 = f32[8,128]{1,0:T(8,128)S(1)} fusion(f32[1664,128,8]{1,0,2:T(8,128)} %get-tuple-element.26, f32[8,128]{1,0:T(8,128)S(1)} %get-tuple-element.9, pred[128,1664]{0,1:T(8,128)(4,1)S(1)} %iota_compare_fusion), kind=kLoop, calls=%fused_computation.19 | loop fusion | flops 8518656 | bytes 7036928 | tf_op jit(solution)/shard_map/reduce_sum | solution.py:39
  43.6 5.4 %all-to-all-start.1 = ((bf16[1,16,8,1024]{3,2,0,1:T(8,128)(2,1)}), bf16[1,16,8,1024]{3,2,0,1:T(8,128)(2,1)S(1)}, u32[]{:S(2)}, u32[]{:S(2)}) async-start(bf16[1,16,8,1024]{3,2,0,1:T(8,128)(2,1)} %bitcast.157), calls=%async_computation.2 | async-start | bytes 524288 | tf_op jit(solution)/shard_map/all_to_all | solution.py:98
  50.9 8.1 %all-to-all-done.1 = bf16[1,16,8,1024]{3,2,0,1:T(8,128)(2,1)S(1)} async-done(((bf16[1,16,8,1024]{3,2,0,1:T(8,128)(2,1)}), bf16[1,16,8,1024]{3,2,0,1:T(8,128)(2,1)S(1)}, u32[]{:S(2)}, u32[]{:S(2)}) %all-to-all-start.1) | async-done | bytes 262176 | tf_op jit(solution)/shard_map/all_to_all | solution.py:98
  64.3 3.9 %collective-permute-done.15 = bf16[64,2048]{1,0:T(8,128)(2,1)S(1)} collective-permute-done((bf16[64,2048]{1,0:T(8,128)(2,1)S(1)}, bf16[64,2048]{1,0:T(8,128)(2,1)S(1)}, u32[]{:S(2)}, u32[]{:S(2)}) %collective-permute-start.15) | collective-permute-done | bytes 262176 | tf_op jit(solution)/shard_map/ppermute | solution.py:14
  68.1 4.6 %collective-permute-start.16 = (bf16[64,2048]{1,0:T(8,128)(2,1)S(1)}, bf16[64,2048]{1,0:T(8,128)(2,1)S(1)}, u32[]{:S(2)}, u32[]{:S(2)}) collective-permute-start(bf16[64,2048]{1,0:T(8,128)(2,1)S(1)} %collective-permute-done.15), channel_id=1, source_target_pairs={{0,15},{1,0},{2,1},{3,2},{4,3},{5,4},{6,5},{7,6},{8,7},{9,8},{10,9... | collective-permute-start | bytes 786440 | tf_op jit(solution)/shard_map/ppermute | solution.py:14
  72.8 3.9 %collective-permute-done.16 = bf16[64,2048]{1,0:T(8,128)(2,1)S(1)} collective-permute-done((bf16[64,2048]{1,0:T(8,128)(2,1)S(1)}, bf16[64,2048]{1,0:T(8,128)(2,1)S(1)}, u32[]{:S(2)}, u32[]{:S(2)}) %collective-permute-start.16) | collective-permute-done | bytes 262176 | tf_op jit(solution)/shard_map/ppermute | solution.py:14
  76.6 4.6 %collective-permute-start.17 = (bf16[64,2048]{1,0:T(8,128)(2,1)S(1)}, bf16[64,2048]{1,0:T(8,128)(2,1)S(1)}, u32[]{:S(2)}, u32[]{:S(2)}) collective-permute-start(bf16[64,2048]{1,0:T(8,128)(2,1)S(1)} %collective-permute-done.16), channel_id=1, source_target_pairs={{0,15},{1,0},{2,1},{3,2},{4,3},{5,4},{6,5},{7,6},{8,7},{9,8},{10,9... | collective-permute-start | bytes 786440 | tf_op jit(solution)/shard_map/ppermute | solution.py:14
  81.3 3.9 collective-permute-done.17
  85.1 4.6 %collective-permute-start.18 = (bf16[64,2048]{1,0:T(8,128)(2,1)S(1)}, bf16[64,2048]{1,0:T(8,128)(2,1)S(1)}, u32[]{:S(2)}, u32[]{:S(2)}) collective-permute-start(bf16[64,2048]{1,0:T(8,128)(2,1)S(1)} %collective-permute-done.17), channel_id=1, source_target_pairs={{0,15},{1,0},{2,1},{3,2},{4,3},{5,4},{6,5},{7,6},{8,7},{9,8},{10,9... | collective-permute-start | bytes 786440 | tf_op jit(solution)/shard_map/ppermute | solution.py:14
  93.6 4.6 %collective-permute-start.19 = (bf16[64,2048]{1,0:T(8,128)(2,1)S(1)}, bf16[64,2048]{1,0:T(8,128)(2,1)}, u32[]{:S(2)}, u32[]{:S(2)}) collective-permute-start(bf16[64,2048]{1,0:T(8,128)(2,1)S(1)} %collective-permute-done.18), channel_id=1, source_target_pairs={{0,15},{1,0},{2,1},{3,2},{4,3},{5,4},{6,5},{7,6},{8,7},{9,8},{10,9... | collective-permute-start | bytes 786440 | tf_op jit(solution)/shard_map/ppermute | solution.py:14
  102.1 4.7 %collective-permute-start.20 = (bf16[64,2048]{1,0:T(8,128)(2,1)}, bf16[64,2048]{1,0:T(8,128)(2,1)}, u32[]{:S(2)}, u32[]{:S(2)}) collective-permute-start(bf16[64,2048]{1,0:T(8,128)(2,1)} %collective-permute-done.19), channel_id=1, source_target_pairs={{0,15},{1,0},{2,1},{3,2},{4,3},{5,4},{6,5},{7,6},{8,7},{9,8},{10,9... | collective-permute-start | bytes 786440 | tf_op jit(solution)/shard_map/ppermute | solution.py:14
  111.0 4.7 %collective-permute-start.21 = (bf16[64,2048]{1,0:T(8,128)(2,1)}, bf16[64,2048]{1,0:T(8,128)(2,1)}, u32[]{:S(2)}, u32[]{:S(2)}) collective-permute-start(bf16[64,2048]{1,0:T(8,128)(2,1)} %collective-permute-done.20), channel_id=1, source_target_pairs={{0,15},{1,0},{2,1},{3,2},{4,3},{5,4},{6,5},{7,6},{8,7},{9,8},{10,9... | collective-permute-start | bytes 786440 | tf_op jit(solution)/shard_map/ppermute | solution.py:14
  115.8 23.8 %all_gather.3 = f32[2,1024,16]{2,0,1:T(2,128)S(1)} all-gather(f32[2,64,16]{2,0,1:T(2,128)S(1)} %copy.50), channel_id=1, replica_groups=mesh['groups'=2,'dev'=16] {'dev'}, dimensions={1}, use_global_device_ids=true | all-gather | bytes 139264 | tf_op jit(solution)/shard_map/all_gather | solution.py:89
  147.8 4.6 %collective-permute-start.23 = (bf16[64,2048]{1,0:T(8,128)(2,1)}, bf16[64,2048]{1,0:T(8,128)(2,1)S(1)}, u32[]{:S(2)}, u32[]{:S(2)}) collective-permute-start(bf16[64,2048]{1,0:T(8,128)(2,1)} %collective-permute-done.22), channel_id=1, source_target_pairs={{0,15},{1,0},{2,1},{3,2},{4,3},{5,4},{6,5},{7,6},{8,7},{9,8},{10,9... | collective-permute-start | bytes 786440 | tf_op jit(solution)/shard_map/ppermute | solution.py:14
  156.6 4.5 %collective-permute-start.24 = (bf16[64,2048]{1,0:T(8,128)(2,1)S(1)}, bf16[64,2048]{1,0:T(8,128)(2,1)S(1)}, u32[]{:S(2)}, u32[]{:S(2)}) collective-permute-start(bf16[64,2048]{1,0:T(8,128)(2,1)S(1)} %collective-permute-done.23), channel_id=1, source_target_pairs={{0,15},{1,0},{2,1},{3,2},{4,3},{5,4},{6,5},{7,6},{8,7},{9,8},{10,9... | collective-permute-start | bytes 786440 | tf_op jit(solution)/shard_map/ppermute | solution.py:14
  190.5 4.6 %collective-permute-start.28 = (bf16[64,2048]{1,0:T(8,128)(2,1)S(1)}, bf16[64,2048]{1,0:T(8,128)(2,1)S(1)}, u32[]{:S(2)}, u32[]{:S(2)}) collective-permute-start(bf16[64,2048]{1,0:T(8,128)(2,1)S(1)} %collective-permute-done.27), channel_id=1, source_target_pairs={{0,15},{1,0},{2,1},{3,2},{4,3},{5,4},{6,5},{7,6},{8,7},{9,8},{10,9... | collective-permute-start | bytes 786440 | tf_op jit(solution)/shard_map/ppermute | solution.py:14
  199.0 4.6 %collective-permute-start.29 = (bf16[64,2048]{1,0:T(8,128)(2,1)S(1)}, bf16[64,2048]{1,0:T(8,128)(2,1)S(1)}, u32[]{:S(2)}, u32[]{:S(2)}) collective-permute-start(bf16[64,2048]{1,0:T(8,128)(2,1)S(1)} %collective-permute-done.28), channel_id=1, source_target_pairs={{0,15},{1,0},{2,1},{3,2},{4,3},{5,4},{6,5},{7,6},{8,7},{9,8},{10,9... | collective-permute-start | bytes 786440 | tf_op jit(solution)/shard_map/ppermute | solution.py:14
  208.2 10.3 %fusion = f32[1024,1536]{1,0:T(8,128)S(1)} fusion(bf16[1,2048,1536]{2,1,0:T(8,128)(2,1)} %param.14, s32[]{:T(128)S(6)} %select_n.40, bf16[1024,2048]{1,0:T(8,128)(2,1)} %constant_dynamic-update-slice_fusion.16), kind=kOutput, calls=%fused_computation.12 | convolution fusion | flops 6450839552 | bytes 16777220 | tf_op jit(solution)/shard_map/dot_general | solution.py:70
  218.6 5.2 %multiply_convert_fusion = bf16[1024,2048]{1,0:T(8,128)(2,1)} fusion(f32[1024]{0:T(1024)S(1)} %bitcast.160, bf16[1,768,2048]{2,1,0:T(8,128)(2,1)S(1)} %copy-done, f32[1024,1536]{1,0:T(8,128)S(1)} %fusion), kind=kOutput, calls=%fused_computation.4 | convolution fusion | flops 3230138368 | bytes 13635584 | tf_op jit(solution)/shard_map/dot_general | solution.py:74
  226.3 4.6 %collective-permute-start.9 = (bf16[64,2048]{1,0:T(8,128)(2,1)}, bf16[64,2048]{1,0:T(8,128)(2,1)S(1)}, u32[]{:S(2)}, u32[]{:S(2)}) collective-permute-start(bf16[64,2048]{1,0:T(8,128)(2,1)} %collective-permute-done.8), channel_id=1, source_target_pairs={{0,15},{1,0},{2,1},{3,2},{4,3},{5,4},{6,5},{7,6},{8,7},{9,8},{10,9... | collective-permute-start | bytes 786440 | tf_op jit(solution)/shard_map/ppermute | solution.py:14
  235.1 4.5 %collective-permute-start.10 = (bf16[64,2048]{1,0:T(8,128)(2,1)S(1)}, bf16[64,2048]{1,0:T(8,128)(2,1)S(1)}, u32[]{:S(2)}, u32[]{:S(2)}) collective-permute-start(bf16[64,2048]{1,0:T(8,128)(2,1)S(1)} %collective-permute-done.9), channel_id=1, source_target_pairs={{0,15},{1,0},{2,1},{3,2},{4,3},{5,4},{6,5},{7,6},{8,7},{9,8},{10,9... | collective-permute-start | bytes 786440 | tf_op jit(solution)/shard_map/ppermute | solution.py:14
  243.5 4.6 %collective-permute-start.11 = (bf16[64,2048]{1,0:T(8,128)(2,1)S(1)}, bf16[64,2048]{1,0:T(8,128)(2,1)S(1)}, u32[]{:S(2)}, u32[]{:S(2)}) collective-permute-start(bf16[64,2048]{1,0:T(8,128)(2,1)S(1)} %collective-permute-done.10), channel_id=1, source_target_pairs={{0,15},{1,0},{2,1},{3,2},{4,3},{5,4},{6,5},{7,6},{8,7},{9,8},{10,9... | collective-permute-start | bytes 786440 | tf_op jit(solution)/shard_map/ppermute | solution.py:14
  252.0 4.6 %collective-permute-start.12 = (bf16[64,2048]{1,0:T(8,128)(2,1)S(1)}, bf16[64,2048]{1,0:T(8,128)(2,1)S(1)}, u32[]{:S(2)}, u32[]{:S(2)}) collective-permute-start(bf16[64,2048]{1,0:T(8,128)(2,1)S(1)} %collective-permute-done.11), channel_id=1, source_target_pairs={{0,15},{1,0},{2,1},{3,2},{4,3},{5,4},{6,5},{7,6},{8,7},{9,8},{10,9... | collective-permute-start | bytes 786440 | tf_op jit(solution)/shard_map/ppermute | solution.py:14
  259.0 5.3 %collective-permute-done.12 = bf16[64,2048]{1,0:T(8,128)(2,1)S(1)} collective-permute-done((bf16[64,2048]{1,0:T(8,128)(2,1)S(1)}, bf16[64,2048]{1,0:T(8,128)(2,1)S(1)}, u32[]{:S(2)}, u32[]{:S(2)}) %collective-permute-start.12) | collective-permute-done | bytes 262176 | tf_op jit(solution)/shard_map/ppermute | solution.py:14
  264.3 4.7 %collective-permute-start.13 = (bf16[64,2048]{1,0:T(8,128)(2,1)S(1)}, bf16[64,2048]{1,0:T(8,128)(2,1)S(1)}, u32[]{:S(2)}, u32[]{:S(2)}) collective-permute-start(bf16[64,2048]{1,0:T(8,128)(2,1)S(1)} %collective-permute-done.12), channel_id=1, source_target_pairs={{0,15},{1,0},{2,1},{3,2},{4,3},{5,4},{6,5},{7,6},{8,7},{9,8},{10,9... | collective-permute-start | bytes 786440 | tf_op jit(solution)/shard_map/ppermute | solution.py:14
  270.5 6.0 %collective-permute-done.13 = bf16[64,2048]{1,0:T(8,128)(2,1)S(1)} collective-permute-done((bf16[64,2048]{1,0:T(8,128)(2,1)S(1)}, bf16[64,2048]{1,0:T(8,128)(2,1)S(1)}, u32[]{:S(2)}, u32[]{:S(2)}) %collective-permute-start.13) | collective-permute-done | bytes 262176 | tf_op jit(solution)/shard_map/ppermute | solution.py:14
  276.4 4.6 %collective-permute-start.14 = (bf16[64,2048]{1,0:T(8,128)(2,1)S(1)}, bf16[64,2048]{1,0:T(8,128)(2,1)S(1)}, u32[]{:S(2)}, u32[]{:S(2)}) collective-permute-start(bf16[64,2048]{1,0:T(8,128)(2,1)S(1)} %collective-permute-done.13), channel_id=1, source_target_pairs={{0,15},{1,0},{2,1},{3,2},{4,3},{5,4},{6,5},{7,6},{8,7},{9,8},{10,9... | collective-permute-start | bytes 786440 | tf_op jit(solution)/shard_map/ppermute | solution.py:14
  285.7 10.5 %fusion.2 = f32[1024,1536]{1,0:T(8,128)S(1)} fusion(bf16[1,2048,1536]{2,1,0:T(8,128)(2,1)} %param.14, s32[]{:T(128)S(6)} %select_n.40, bf16[1024,2048]{1,0:T(8,128)(2,1)} %constant_dynamic-update-slice_fusion), kind=kOutput, calls=%fused_computation.14 | convolution fusion | flops 6450839552 | bytes 16777220 | tf_op jit(solution)/shard_map/dot_general | solution.py:70
  296.2 5.1 %multiply_convert_fusion.1 = bf16[1024,2048]{1,0:T(8,128)(2,1)} fusion(f32[1024]{0:T(1024)S(1)} %bitcast.159, bf16[1,768,2048]{2,1,0:T(8,128)(2,1)S(1)} %copy-done, f32[1024,1536]{1,0:T(8,128)S(1)} %fusion.2), kind=kOutput, calls=%fused_computation.5 | convolution fusion | flops 3230138368 | bytes 13635584 | tf_op jit(solution)/shard_map/dot_general | solution.py:74
  301.4 75.7 %reduce-scatter.3.cloned.1.call-done = bf16[64,2048]{1,0:T(8,128)(2,1)} async-done(((bf16[1024,2048]{1,0:T(8,128)(2,1)}), bf16[64,2048]{1,0:T(8,128)(2,1)}) %reduce-scatter.3.cloned.1.call-update) | async-done | bytes 262160 | tf_op jit(solution)/shard_map/reduce_scatter | solution.py:103
  (131 shorter events, 115.0 us)
Async XLA Ops:
  26.0 17.5 %all-to-all-start = ((bf16[1,16,8,1024]{3,2,0,1:T(8,128)(2,1)}), bf16[1,16,8,1024]{3,2,0,1:T(8,128)(2,1)}, u32[]{:S(2)}, u32[]{:S(2)}) async-start(bf16[1,16,8,1024]{3,2,0,1:T(8,128)(2,1)} %bitcast.156), calls=%async_computation | async-start | bytes 524288 | tf_op jit(solution)/shard_map/all_to_all | solution.py:98
  43.6 15.4 %all-to-all-start.1 = ((bf16[1,16,8,1024]{3,2,0,1:T(8,128)(2,1)}), bf16[1,16,8,1024]{3,2,0,1:T(8,128)(2,1)S(1)}, u32[]{:S(2)}, u32[]{:S(2)}) async-start(bf16[1,16,8,1024]{3,2,0,1:T(8,128)(2,1)} %bitcast.157), calls=%async_computation.2 | async-start | bytes 524288 | tf_op jit(solution)/shard_map/all_to_all | solution.py:98
  49.0 252.4 %reduce-scatter.5.cloned.1.call-start = ((), (), s32[]{:S(2)}) async-start(), calls=%async_computation.5 | async-start | bytes 4456448 | tf_op jit(solution)/shard_map/reduce_scatter | solution.py:103
  68.1 8.5 %collective-permute-start.16 = (bf16[64,2048]{1,0:T(8,128)(2,1)S(1)}, bf16[64,2048]{1,0:T(8,128)(2,1)S(1)}, u32[]{:S(2)}, u32[]{:S(2)}) collective-permute-start(bf16[64,2048]{1,0:T(8,128)(2,1)S(1)} %collective-permute-done.15), channel_id=1, source_target_pairs={{0,15},{1,0},{2,1},{3,2},{4,3},{5,4},{6,5},{7,6},{8,7},{9,8},{10,9... | collective-permute-start | bytes 786440 | tf_op jit(solution)/shard_map/ppermute | solution.py:14
  76.6 8.5 %collective-permute-start.17 = (bf16[64,2048]{1,0:T(8,128)(2,1)S(1)}, bf16[64,2048]{1,0:T(8,128)(2,1)S(1)}, u32[]{:S(2)}, u32[]{:S(2)}) collective-permute-start(bf16[64,2048]{1,0:T(8,128)(2,1)S(1)} %collective-permute-done.16), channel_id=1, source_target_pairs={{0,15},{1,0},{2,1},{3,2},{4,3},{5,4},{6,5},{7,6},{8,7},{9,8},{10,9... | collective-permute-start | bytes 786440 | tf_op jit(solution)/shard_map/ppermute | solution.py:14
  81.2 8.5 %collective-permute-start = (bf16[64,2048]{1,0:T(8,128)(2,1)S(1)}, bf16[64,2048]{1,0:T(8,128)(2,1)S(1)}, u32[]{:S(2)}, u32[]{:S(2)}) collective-permute-start(bf16[64,2048]{1,0:T(8,128)(2,1)S(1)} %get-tuple-element.11), channel_id=1, source_target_pairs={{0,15},{1,0},{2,1},{3,2},{4,3},{5,4},{6,5},{7,6},{8,7},{9,8},{10,9... | collective-permute-start | bytes 786440 | tf_op jit(solution)/shard_map/ppermute | solution.py:14
  85.1 8.5 %collective-permute-start.18 = (bf16[64,2048]{1,0:T(8,128)(2,1)S(1)}, bf16[64,2048]{1,0:T(8,128)(2,1)S(1)}, u32[]{:S(2)}, u32[]{:S(2)}) collective-permute-start(bf16[64,2048]{1,0:T(8,128)(2,1)S(1)} %collective-permute-done.17), channel_id=1, source_target_pairs={{0,15},{1,0},{2,1},{3,2},{4,3},{5,4},{6,5},{7,6},{8,7},{9,8},{10,9... | collective-permute-start | bytes 786440 | tf_op jit(solution)/shard_map/ppermute | solution.py:14
  89.7 8.5 %collective-permute-start.1 = (bf16[64,2048]{1,0:T(8,128)(2,1)S(1)}, bf16[64,2048]{1,0:T(8,128)(2,1)}, u32[]{:S(2)}, u32[]{:S(2)}) collective-permute-start(bf16[64,2048]{1,0:T(8,128)(2,1)S(1)} %collective-permute-done), channel_id=1, source_target_pairs={{0,15},{1,0},{2,1},{3,2},{4,3},{5,4},{6,5},{7,6},{8,7},{9,8},{10,9... | collective-permute-start | bytes 786440 | tf_op jit(solution)/shard_map/ppermute | solution.py:14
  93.6 8.5 %collective-permute-start.19 = (bf16[64,2048]{1,0:T(8,128)(2,1)S(1)}, bf16[64,2048]{1,0:T(8,128)(2,1)}, u32[]{:S(2)}, u32[]{:S(2)}) collective-permute-start(bf16[64,2048]{1,0:T(8,128)(2,1)S(1)} %collective-permute-done.18), channel_id=1, source_target_pairs={{0,15},{1,0},{2,1},{3,2},{4,3},{5,4},{6,5},{7,6},{8,7},{9,8},{10,9... | collective-permute-start | bytes 786440 | tf_op jit(solution)/shard_map/ppermute | solution.py:14
  98.2 8.8 %collective-permute-start.2 = (bf16[64,2048]{1,0:T(8,128)(2,1)}, bf16[64,2048]{1,0:T(8,128)(2,1)}, u32[]{:S(2)}, u32[]{:S(2)}) collective-permute-start(bf16[64,2048]{1,0:T(8,128)(2,1)} %collective-permute-done.1), channel_id=1, source_target_pairs={{0,15},{1,0},{2,1},{3,2},{4,3},{5,4},{6,5},{7,6},{8,7},{9,8},{10,9... | collective-permute-start | bytes 786440 | tf_op jit(solution)/shard_map/ppermute | solution.py:14
  102.1 8.9 %collective-permute-start.20 = (bf16[64,2048]{1,0:T(8,128)(2,1)}, bf16[64,2048]{1,0:T(8,128)(2,1)}, u32[]{:S(2)}, u32[]{:S(2)}) collective-permute-start(bf16[64,2048]{1,0:T(8,128)(2,1)} %collective-permute-done.19), channel_id=1, source_target_pairs={{0,15},{1,0},{2,1},{3,2},{4,3},{5,4},{6,5},{7,6},{8,7},{9,8},{10,9... | collective-permute-start | bytes 786440 | tf_op jit(solution)/shard_map/ppermute | solution.py:14
  107.0 33.7 %collective-permute-start.3 = (bf16[64,2048]{1,0:T(8,128)(2,1)}, bf16[64,2048]{1,0:T(8,128)(2,1)}, u32[]{:S(2)}, u32[]{:S(2)}) collective-permute-start(bf16[64,2048]{1,0:T(8,128)(2,1)} %collective-permute-done.2), channel_id=1, source_target_pairs={{0,15},{1,0},{2,1},{3,2},{4,3},{5,4},{6,5},{7,6},{8,7},{9,8},{10,9... | collective-permute-start | bytes 786440 | tf_op jit(solution)/shard_map/ppermute | solution.py:14
  111.0 29.8 %collective-permute-start.21 = (bf16[64,2048]{1,0:T(8,128)(2,1)}, bf16[64,2048]{1,0:T(8,128)(2,1)}, u32[]{:S(2)}, u32[]{:S(2)}) collective-permute-start(bf16[64,2048]{1,0:T(8,128)(2,1)} %collective-permute-done.20), channel_id=1, source_target_pairs={{0,15},{1,0},{2,1},{3,2},{4,3},{5,4},{6,5},{7,6},{8,7},{9,8},{10,9... | collective-permute-start | bytes 786440 | tf_op jit(solution)/shard_map/ppermute | solution.py:14
  140.7 13.4 %collective-permute-start.4 = (bf16[64,2048]{1,0:T(8,128)(2,1)}, bf16[64,2048]{1,0:T(8,128)(2,1)}, u32[]{:S(2)}, u32[]{:S(2)}) collective-permute-start(bf16[64,2048]{1,0:T(8,128)(2,1)} %collective-permute-done.3), channel_id=1, source_target_pairs={{0,15},{1,0},{2,1},{3,2},{4,3},{5,4},{6,5},{7,6},{8,7},{9,8},{10,9... | collective-permute-start | bytes 786440 | tf_op jit(solution)/shard_map/ppermute | solution.py:14
  140.8 7.0 %collective-permute-start.22 = (bf16[64,2048]{1,0:T(8,128)(2,1)}, bf16[64,2048]{1,0:T(8,128)(2,1)}, u32[]{:S(2)}, u32[]{:S(2)}) collective-permute-start(bf16[64,2048]{1,0:T(8,128)(2,1)} %collective-permute-done.21), channel_id=1, source_target_pairs={{0,15},{1,0},{2,1},{3,2},{4,3},{5,4},{6,5},{7,6},{8,7},{9,8},{10,9... | collective-permute-start | bytes 786440 | tf_op jit(solution)/shard_map/ppermute | solution.py:14
  147.8 8.8 %collective-permute-start.23 = (bf16[64,2048]{1,0:T(8,128)(2,1)}, bf16[64,2048]{1,0:T(8,128)(2,1)S(1)}, u32[]{:S(2)}, u32[]{:S(2)}) collective-permute-start(bf16[64,2048]{1,0:T(8,128)(2,1)} %collective-permute-done.22), channel_id=1, source_target_pairs={{0,15},{1,0},{2,1},{3,2},{4,3},{5,4},{6,5},{7,6},{8,7},{9,8},{10,9... | collective-permute-start | bytes 786440 | tf_op jit(solution)/shard_map/ppermute | solution.py:14
  154.1 8.7 %collective-permute-start.5 = (bf16[64,2048]{1,0:T(8,128)(2,1)}, bf16[64,2048]{1,0:T(8,128)(2,1)S(1)}, u32[]{:S(2)}, u32[]{:S(2)}) collective-permute-start(bf16[64,2048]{1,0:T(8,128)(2,1)} %collective-permute-done.4), channel_id=1, source_target_pairs={{0,15},{1,0},{2,1},{3,2},{4,3},{5,4},{6,5},{7,6},{8,7},{9,8},{10,9... | collective-permute-start | bytes 786440 | tf_op jit(solution)/shard_map/ppermute | solution.py:14
  156.6 9.7 %collective-permute-start.24 = (bf16[64,2048]{1,0:T(8,128)(2,1)S(1)}, bf16[64,2048]{1,0:T(8,128)(2,1)S(1)}, u32[]{:S(2)}, u32[]{:S(2)}) collective-permute-start(bf16[64,2048]{1,0:T(8,128)(2,1)S(1)} %collective-permute-done.23), channel_id=1, source_target_pairs={{0,15},{1,0},{2,1},{3,2},{4,3},{5,4},{6,5},{7,6},{8,7},{9,8},{10,9... | collective-permute-start | bytes 786440 | tf_op jit(solution)/shard_map/ppermute | solution.py:14
  163.5 7.8 %collective-permute-start.6 = (bf16[64,2048]{1,0:T(8,128)(2,1)S(1)}, bf16[64,2048]{1,0:T(8,128)(2,1)S(1)}, u32[]{:S(2)}, u32[]{:S(2)}) collective-permute-start(bf16[64,2048]{1,0:T(8,128)(2,1)S(1)} %collective-permute-done.5), channel_id=1, source_target_pairs={{0,15},{1,0},{2,1},{3,2},{4,3},{5,4},{6,5},{7,6},{8,7},{9,8},{10,9... | collective-permute-start | bytes 786440 | tf_op jit(solution)/shard_map/ppermute | solution.py:14
  166.3 9.2 %collective-permute-start.25 = (bf16[64,2048]{1,0:T(8,128)(2,1)S(1)}, bf16[64,2048]{1,0:T(8,128)(2,1)S(1)}, u32[]{:S(2)}, u32[]{:S(2)}) collective-permute-start(bf16[64,2048]{1,0:T(8,128)(2,1)S(1)} %collective-permute-done.24), channel_id=1, source_target_pairs={{0,15},{1,0},{2,1},{3,2},{4,3},{5,4},{6,5},{7,6},{8,7},{9,8},{10,9... | collective-permute-start | bytes 786440 | tf_op jit(solution)/shard_map/ppermute | solution.py:14
  172.0 7.8 %collective-permute-start.7 = (bf16[64,2048]{1,0:T(8,128)(2,1)S(1)}, bf16[64,2048]{1,0:T(8,128)(2,1)}, u32[]{:S(2)}, u32[]{:S(2)}) collective-permute-start(bf16[64,2048]{1,0:T(8,128)(2,1)S(1)} %collective-permute-done.6), channel_id=1, source_target_pairs={{0,15},{1,0},{2,1},{3,2},{4,3},{5,4},{6,5},{7,6},{8,7},{9,8},{10,9... | collective-permute-start | bytes 786440 | tf_op jit(solution)/shard_map/ppermute | solution.py:14
  175.5 8.6 %collective-permute-start.26 = (bf16[64,2048]{1,0:T(8,128)(2,1)S(1)}, bf16[64,2048]{1,0:T(8,128)(2,1)S(1)}, u32[]{:S(2)}, u32[]{:S(2)}) collective-permute-start(bf16[64,2048]{1,0:T(8,128)(2,1)S(1)} %collective-permute-done.25), channel_id=1, source_target_pairs={{0,15},{1,0},{2,1},{3,2},{4,3},{5,4},{6,5},{7,6},{8,7},{9,8},{10,9... | collective-permute-start | bytes 786440 | tf_op jit(solution)/shard_map/ppermute | solution.py:14
  179.8 46.5 %collective-permute-start.8 = (bf16[64,2048]{1,0:T(8,128)(2,1)}, bf16[64,2048]{1,0:T(8,128)(2,1)}, u32[]{:S(2)}, u32[]{:S(2)}) collective-permute-start(bf16[64,2048]{1,0:T(8,128)(2,1)} %collective-permute-done.7), channel_id=1, source_target_pairs={{0,15},{1,0},{2,1},{3,2},{4,3},{5,4},{6,5},{7,6},{8,7},{9,8},{10,9... | collective-permute-start | bytes 786440 | tf_op jit(solution)/shard_map/ppermute | solution.py:14
  190.5 8.5 %collective-permute-start.28 = (bf16[64,2048]{1,0:T(8,128)(2,1)S(1)}, bf16[64,2048]{1,0:T(8,128)(2,1)S(1)}, u32[]{:S(2)}, u32[]{:S(2)}) collective-permute-start(bf16[64,2048]{1,0:T(8,128)(2,1)S(1)} %collective-permute-done.27), channel_id=1, source_target_pairs={{0,15},{1,0},{2,1},{3,2},{4,3},{5,4},{6,5},{7,6},{8,7},{9,8},{10,9... | collective-permute-start | bytes 786440 | tf_op jit(solution)/shard_map/ppermute | solution.py:14
  199.0 8.5 %collective-permute-start.29 = (bf16[64,2048]{1,0:T(8,128)(2,1)S(1)}, bf16[64,2048]{1,0:T(8,128)(2,1)S(1)}, u32[]{:S(2)}, u32[]{:S(2)}) collective-permute-start(bf16[64,2048]{1,0:T(8,128)(2,1)S(1)} %collective-permute-done.28), channel_id=1, source_target_pairs={{0,15},{1,0},{2,1},{3,2},{4,3},{5,4},{6,5},{7,6},{8,7},{9,8},{10,9... | collective-permute-start | bytes 786440 | tf_op jit(solution)/shard_map/ppermute | solution.py:14
  223.8 153.3 %reduce-scatter.3.cloned.1.call-start = ((), (), s32[]{:S(2)}) async-start(), calls=%async_computation.4 | async-start | bytes 4456448 | tf_op jit(solution)/shard_map/reduce_scatter | solution.py:103
  226.3 8.8 %collective-permute-start.9 = (bf16[64,2048]{1,0:T(8,128)(2,1)}, bf16[64,2048]{1,0:T(8,128)(2,1)S(1)}, u32[]{:S(2)}, u32[]{:S(2)}) collective-permute-start(bf16[64,2048]{1,0:T(8,128)(2,1)} %collective-permute-done.8), channel_id=1, source_target_pairs={{0,15},{1,0},{2,1},{3,2},{4,3},{5,4},{6,5},{7,6},{8,7},{9,8},{10,9... | collective-permute-start | bytes 786440 | tf_op jit(solution)/shard_map/ppermute | solution.py:14
  235.1 8.4 %collective-permute-start.10 = (bf16[64,2048]{1,0:T(8,128)(2,1)S(1)}, bf16[64,2048]{1,0:T(8,128)(2,1)S(1)}, u32[]{:S(2)}, u32[]{:S(2)}) collective-permute-start(bf16[64,2048]{1,0:T(8,128)(2,1)S(1)} %collective-permute-done.9), channel_id=1, source_target_pairs={{0,15},{1,0},{2,1},{3,2},{4,3},{5,4},{6,5},{7,6},{8,7},{9,8},{10,9... | collective-permute-start | bytes 786440 | tf_op jit(solution)/shard_map/ppermute | solution.py:14
  243.5 8.5 %collective-permute-start.11 = (bf16[64,2048]{1,0:T(8,128)(2,1)S(1)}, bf16[64,2048]{1,0:T(8,128)(2,1)S(1)}, u32[]{:S(2)}, u32[]{:S(2)}) collective-permute-start(bf16[64,2048]{1,0:T(8,128)(2,1)S(1)} %collective-permute-done.10), channel_id=1, source_target_pairs={{0,15},{1,0},{2,1},{3,2},{4,3},{5,4},{6,5},{7,6},{8,7},{9,8},{10,9... | collective-permute-start | bytes 786440 | tf_op jit(solution)/shard_map/ppermute | solution.py:14
  252.0 12.4 %collective-permute-start.12 = (bf16[64,2048]{1,0:T(8,128)(2,1)S(1)}, bf16[64,2048]{1,0:T(8,128)(2,1)S(1)}, u32[]{:S(2)}, u32[]{:S(2)}) collective-permute-start(bf16[64,2048]{1,0:T(8,128)(2,1)S(1)} %collective-permute-done.11), channel_id=1, source_target_pairs={{0,15},{1,0},{2,1},{3,2},{4,3},{5,4},{6,5},{7,6},{8,7},{9,8},{10,9... | collective-permute-start | bytes 786440 | tf_op jit(solution)/shard_map/ppermute | solution.py:14
  264.3 12.1 %collective-permute-start.13 = (bf16[64,2048]{1,0:T(8,128)(2,1)S(1)}, bf16[64,2048]{1,0:T(8,128)(2,1)S(1)}, u32[]{:S(2)}, u32[]{:S(2)}) collective-permute-start(bf16[64,2048]{1,0:T(8,128)(2,1)S(1)} %collective-permute-done.12), channel_id=1, source_target_pairs={{0,15},{1,0},{2,1},{3,2},{4,3},{5,4},{6,5},{7,6},{8,7},{9,8},{10,9... | collective-permute-start | bytes 786440 | tf_op jit(solution)/shard_map/ppermute | solution.py:14
  276.4 8.5 %collective-permute-start.14 = (bf16[64,2048]{1,0:T(8,128)(2,1)S(1)}, bf16[64,2048]{1,0:T(8,128)(2,1)S(1)}, u32[]{:S(2)}, u32[]{:S(2)}) collective-permute-start(bf16[64,2048]{1,0:T(8,128)(2,1)S(1)} %collective-permute-done.13), channel_id=1, source_target_pairs={{0,15},{1,0},{2,1},{3,2},{4,3},{5,4},{6,5},{7,6},{8,7},{9,8},{10,9... | collective-permute-start | bytes 786440 | tf_op jit(solution)/shard_map/ppermute | solution.py:14
  (16 other events, 414.6 us)
Sparse Core Ops, SparseCore 0:
  223.9 77.4 reduce-scatter.4
  305.2 71.8 reduce-scatter.2
